TPU v7x, 32 devices: a whole 2x2x4 slice. The times are simulated.
32 devices in a mesh: group: 2 (over x), ctx: 8 (over z, y), tp: 2 (over core).
Axes of the slice: x: 2, y: 2, z: 4, core: 2. Of those that a mesh axis runs over, the one named last changes fastest.
Arguments:
- query_proj: bfloat16 [2048, 8192], P(('group', 'ctx'), 'tp'), parts along dimension 0, may hold values from -6 to 6
- key_proj: bfloat16 [2048, 8192], P(('group', 'ctx'), 'tp'), parts along dimension 0, may hold values from -6 to 6
- value_proj: bfloat16 [2048, 8192], P(('group', 'ctx'), 'tp'), parts along dimension 0, may hold values from -6 to 6
- genome_ids: int32 [2048], P('group'), parts along dimension 0, may hold values from 0 to 3, never falling along the last dimension, each value on 1 to 512 neighbouring positions
- filters: float32 [512, 128], P('tp'), may hold values from -0.5 to 0.5
- out_weight: bfloat16 [8192, 8192], P('tp', 'ctx'), may hold values from -0.0625 to 0.0625
- out_grad: bfloat16 [2048, 8192], P(('group', 'ctx'), 'tp'), parts along dimension 0, may hold values from -6 to 6
Outputs:
- query_grad: bfloat16 [2048, 8192], P(('group', 'ctx'), 'tp'), parts along dimension 0
- key_grad: bfloat16 [2048, 8192], P(('group', 'ctx'), 'tp'), parts along dimension 0
- value_grad: bfloat16 [2048, 8192], P(('group', 'ctx'), 'tp'), parts along dimension 0
- filter_grad: float32 [1024, 128], P(('group', 'tp')), parts along dimension 0
There are 2 independent parts, one for each index of `group`. A program takes and returns all parts, laid end to end along the dimension named above; an argument that names none is the same for every part. Nothing has to cross between parts.
Inputs may be any that keep to these rules, and one draw needn't show every extreme that they name: `genome_ids`: genome ids never fall along the rows; every genome covers 1 to 512 consecutive rows, and one covers exactly 512.
All inputs are finite; a program needn't handle non-finite values.
Results may differ from a plain program's by a relative error of at most 0.017.
Values may be sent and summed in bfloat16 or wider, within the bound.
A program may use at most 192 MiB of HBM per device.

v0:
```python
import jax
import jax.numpy as jnp
import numpy as np
from jax import lax
from jax.sharding import PartitionSpec as P


def from_behind(array, axis, by):
    length = lax.axis_size(axis)
    pairs = [(i, i + by) for i in range(length) if 0 <= i + by < length]
    return lax.ppermute(array, axis, pairs)


def rounded(source):
    return lax.optimization_barrier(source.astype(jnp.bfloat16)).astype(jnp.float32)


def lag_tables(filt_vals, tap_count):
    row_pos = np.arange(tap_count)[:, None]
    col_pos = np.arange(2 * tap_count)[None, :]
    tables = []
    for offsets in (row_pos + tap_count - col_pos, col_pos - row_pos):
        inside = (offsets >= 0) & (offsets < tap_count)
        picked = jnp.take(filt_vals, np.clip(offsets, 0, tap_count - 1).reshape(-1), axis=1)
        picked = picked.reshape(filt_vals.shape[0], tap_count, 2 * tap_count)
        tables.append(jnp.where(inside[None], picked, jnp.zeros_like(picked)))
    return (tables[0], tables[1])


def fold_lags(product, tap_count):
    group_count = product.shape[0]
    flat = product.reshape(group_count, 2 * tap_count * tap_count)
    flat = jnp.concatenate([flat, jnp.zeros((group_count, tap_count), flat.dtype)], 1)
    skewed = flat.reshape(group_count, tap_count, 2 * tap_count + 1)
    return jnp.flip(jnp.sum(skewed[:, :, 1 : tap_count + 1], axis=1), axis=1)


def per_device(query_proj, key_proj, value_proj, genome_ids, filters, out_weight, out_grad):
    row_count, feature_count = query_proj.shape
    group_local = filters.shape[0]
    chan_count = feature_count // group_local
    tap_count = filters.shape[1]
    first_global = lax.axis_index("ctx") * row_count
    pad_ids = jnp.full((tap_count,), -1, jnp.int32)
    ids_pad = jnp.concatenate([pad_ids, genome_ids, pad_ids])
    key_f32 = key_proj.astype(jnp.float32)
    value_f32 = value_proj.astype(jnp.float32)
    mixed = (key_f32 * value_f32).astype(jnp.bfloat16)
    before = from_behind(mixed, "ctx", 1)
    mixed_ext = jnp.concatenate([before, mixed], 0)
    fwd_table, back_table = lag_tables(filters.astype(jnp.bfloat16), tap_count)
    grad_full = lax.all_gather(out_grad, "tp", axis=1, tiled=True)
    columns = lax.all_to_all(grad_full, "ctx", split_axis=1, concat_axis=0, tiled=True)
    summed = lax.psum_scatter(
        lax.dot_general(
            columns, out_weight, (((1,), (1,)), ((), ())), preferred_element_type=jnp.float32
        ).astype(jnp.bfloat16),
        "ctx",
        scatter_dimension=0,
        tiled=True,
    ).astype(jnp.float32)
    dz_vals = rounded(summed)
    block_index = 0
    first_row = block_index * tap_count
    window = mixed_ext
    ids_rows = lax.dynamic_slice_in_dim(ids_pad, first_global + first_row + tap_count, tap_count)
    ids_prev = lax.dynamic_slice_in_dim(ids_pad, first_global + first_row, 2 * tap_count)
    ids_next = lax.dynamic_slice_in_dim(
        ids_pad, first_global + first_row + tap_count, 2 * tap_count
    )
    same_prev = (ids_rows[:, None] == ids_prev[None, :]).astype(jnp.bfloat16)
    prev_masks = [same_prev]
    next_masks = [(ids_rows[:, None] == ids_next[None, :]).astype(jnp.bfloat16)]
    block_out = jnp.einsum(
        "gtw,wgc->tgc",
        fwd_table * same_prev[None],
        window.reshape(2 * tap_count, group_local, chan_count),
        preferred_element_type=jnp.float32,
    )
    conv_parts = block_out.reshape(tap_count, feature_count)
    query_grad = (dz_vals * conv_parts).astype(jnp.bfloat16)
    grad_conv = (dz_vals * query_proj.astype(jnp.float32)).astype(jnp.bfloat16)
    after = from_behind(grad_conv, "ctx", -1)
    grad_ext = jnp.concatenate([grad_conv, after], 0)
    block_index = 0
    window = mixed_ext.reshape(2 * tap_count, group_local, chan_count)
    grad_window = grad_ext.reshape(2 * tap_count, group_local, chan_count)
    grad_rows = grad_conv.reshape(tap_count, group_local, chan_count)
    block_grad = jnp.einsum(
        "gtw,wgc->tgc",
        back_table * next_masks[block_index][None],
        grad_window,
        preferred_element_type=jnp.float32,
    )
    grad_parts = block_grad.reshape(tap_count, feature_count)
    product = jnp.einsum("tgc,wgc->gtw", grad_rows, window, preferred_element_type=jnp.float32)
    filt_local = fold_lags(product * prev_masks[block_index].astype(jnp.float32)[None], tap_count)
    key_grad = (grad_parts * value_f32).astype(jnp.bfloat16)
    value_grad = (grad_parts * key_f32).astype(jnp.bfloat16)
    filter_grad = lax.psum(filt_local.astype(jnp.bfloat16), "ctx").astype(jnp.float32)
    return (query_grad, key_grad, value_grad, filter_grad)


def solution(mesh):
    in_specs = (
        P(("group", "ctx"), "tp"),
        P(("group", "ctx"), "tp"),
        P(("group", "ctx"), "tp"),
        P("group"),
        P("tp", None),
        P("tp", "ctx"),
        P(("group", "ctx"), "tp"),
    )
    out_specs = (
        P(("group", "ctx"), "tp"),
        P(("group", "ctx"), "tp"),
        P(("group", "ctx"), "tp"),
        P(("group", "tp"), None),
    )
    return jax.shard_map(
        per_device, mesh=mesh, in_specs=in_specs, out_specs=out_specs, check_vma=False
    )
```

profile of v0, /device:TPU:0, one launch (start us, length us, event | category | flops | bytes accessed | tf_op | source)
XLA Modules:
  0.0 785.1 jit_solution(3224054432893824704)
XLA Ops:
  7.2 2.3 copy.46
  9.5 13.9 %all-gather.2.cloned.1.call-done = bf16[128,8192]{0,1:T(8,128)(2,1)} async-done(((bf16[128,4096]{0,1:T(8,128)(2,1)}), bf16[128,8192]{0,1:T(8,128)(2,1)}) %all-gather.2.cloned.1.call-update) | async-done | bytes 2097168 | tf_op jit(solution)/shard_map/all_gather | solution.py:52
  23.4 54.4 %all_to_all.19 = bf16[128,8,1024]{0,2,1:T(8,128)(2,1)S(1)} all-to-all(bf16[128,8,1024]{0,2,1:T(8,128)(2,1)} %bitcast.34), channel_id=1, replica_groups=mesh['group'=2,'ctx'=8,'tp'=2] {'ctx'}, dimensions={1} | all-to-all | bytes 4194304 | tf_op jit(solution)/shard_map/all_to_all | solution.py:53
  77.9 2.7 copy.47
  80.5 14.8 %convolution_convert_fusion = bf16[1024,4096]{1,0:T(8,128)(2,1)} fusion(bf16[1024,1024]{1,0:T(8,128)(2,1)} %bitcast.38, bf16[4096,1024]{1,0:T(8,128)(2,1)} %param.18), kind=kOutput, calls=%fused_computation.16 | convolution fusion | flops 8594128896 | bytes 18874368 | tf_op jit(solution)/shard_map/dot_general | solution.py:55
  95.4 0.7 copy-done.7
  96.4 147.2 %reduce-scatter.2.cloned.1.call-done = bf16[128,4096]{1,0:T(8,128)(2,1)} async-done(((bf16[1024,4096]{1,0:T(8,128)(2,1)}), bf16[128,4096]{1,0:T(8,128)(2,1)}) %reduce-scatter.2.cloned.1.call-update) | async-done | bytes 1048592 | tf_op jit(solution)/shard_map/reduce_scatter | solution.py:54
  243.5 1.5 fusion.13
  245.0 1.3 collective-permute-start.1
  246.4 129.4 %gather_fusion.1 = bf16[32768,256]{1,0:T(8,128)(2,1)} fusion(bf16[256,128]{0,1:T(8,128)(2,1)S(1)} %copy.49, s32[32768]{0:T(1024)S(1)} %broadcast_clamp_fusion), kind=kCustom, calls=%fused_computation.1.clone | custom fusion | bytes 33685504 | tf_op jit(solution)/shard_map/jit(_take)/gather | solution.py:24
  375.8 23.5 %copy.53 = bf16[256,128,256]{2,1,0:T(8,128)(2,1)} copy(bf16[256,128,256]{0,2,1:T(8,128)(2,1)} %bitcast.29) | data formatting | bytes 33554432 | tf_op jit(solution)/shard_map/reshape | solution.py:25
  399.6 1.4 pad_maximum_fusion.1
  401.0 2.5 copy.52
  403.4 12.2 %fusion = f32[256,16,128]{2,1,0:T(8,128)} fusion(bf16[256,256,16]{0,2,1:T(8,128)(2,1)} %bitcast.35, bf16[256,128,256]{2,1,0:T(8,128)(2,1)} %copy.53, pred[128,256]{1,0:T(8,128)(4,1)S(1)} %copy.61, bf16[128,256]{1,0:T(8,128)(2,1)S(1)} %get-tuple-element.16), kind=kOutput, calls=%fused_computation.4 | convolution fusion | flops 285212672 | bytes 21069824 | tf_op jit(solution)/shard_map/gtw,wgc->tgc/dot_general | solution.py:89
  415.6 1.9 copy.54
  417.6 3.7 fusion.14
  421.3 5.5 collective-permute-start
  426.9 129.4 %gather_fusion = bf16[32768,256]{1,0:T(8,128)(2,1)} fusion(bf16[256,128]{0,1:T(8,128)(2,1)S(1)} %copy.49, s32[32768]{0:T(1024)S(1)} %broadcast_clamp_fusion.1), kind=kCustom, calls=%fused_computation.clone | custom fusion | bytes 33685504 | tf_op jit(solution)/shard_map/jit(_take)/gather | solution.py:24
  556.4 23.5 %copy.50 = bf16[256,128,256]{2,1,0:T(8,128)(2,1)} copy(bf16[256,128,256]{0,2,1:T(8,128)(2,1)} %bitcast.28) | data formatting | bytes 33554432 | tf_op jit(solution)/shard_map/reshape | solution.py:25
  580.5 3.1 pad_maximum_fusion
  583.6 3.3 copy.48
  586.9 11.6 %fusion.3 = f32[256,16,128]{2,1,0:T(8,128)} fusion(bf16[256,256,16]{0,2,1:T(8,128)(2,1)S(1)} %bitcast.30, bf16[256,128,256]{2,1,0:T(8,128)(2,1)} %copy.50, pred[128,256]{1,0:T(8,128)(4,1)S(1)} %copy.62, bf16[128,256]{1,0:T(8,128)(2,1)S(1)} %get-tuple-element.15), kind=kOutput, calls=%fused_computation.7 | convolution fusion | flops 285212672 | bytes 21069824 | tf_op jit(solution)/shard_map/gtw,wgc->tgc/dot_general | solution.py:74
  598.5 3.0 copy.51
  601.5 13.1 %broadcast_multiply_fusion = f32[256,128,256]{2,1,0:T(8,128)} fusion(f32[128,256]{1,0:T(8,128)S(1)} %get-tuple-element.14, bf16[128,256,16]{0,2,1:T(8,128)(2,1)S(1)} %bitcast.33, bf16[256,256,16]{0,2,1:T(8,128)(2,1)S(1)} %bitcast.31), kind=kOutput, calls=%fused_computation.3 | convolution fusion | flops 276824064 | bytes 36831232 | tf_op jit(solution)/shard_map/tgc,wgc->gtw/dot_general | solution.py:96
  614.6 35.0 %copy.59 = f32[256,128,256]{0,2,1:T(8,128)} copy(f32[256,128,256]{2,1,0:T(8,128)} %broadcast_multiply_fusion) | data formatting | bytes 67108864 | tf_op jit(solution)/shard_map/reshape | solution.py:32
  649.6 22.4 %concatenate.15 = f32[256,32896]{0,1:T(8,128)} pad(f32[256,32768]{0,1:T(8,128)} %bitcast.27, f32[]{:T(128)} %constant.38.clone.1), padding=0_0x0_128 | pad | bytes 67239936 | tf_op jit(solution)/shard_map/concatenate | solution.py:33
  672.0 28.3 %reshape.129 = f32[256,128,257]{0,2,1:T(8,128)} reshape(f32[256,32896]{0,1:T(8,128)} %concatenate.15) | data formatting | bytes 67371008 | tf_op jit(solution)/shard_map/reshape | solution.py:34
  700.3 8.4 %slice_reduce_fusion = bf16[256,128]{0,1:T(8,128)(2,1)S(1)} fusion(f32[256,128,257]{0,2,1:T(8,128)} %reshape.129), kind=kLoop, calls=%fused_computation.2 | loop fusion | flops 4161536 | bytes 16842752 | tf_op jit(solution)/shard_map/reduce_sum | solution.py:35
  708.6 0.7 rev.4
  709.3 1.2 fusion.12
  710.5 66.4 %all-reduce.3.cloned.1.call-done = bf16[256,128]{0,1:T(8,128)(2,1)} async-done(((bf16[256,128]{0,1:T(8,128)(2,1)}), bf16[256,128]{0,1:T(8,128)(2,1)}) %all-reduce.3.cloned.1.call-update) | async-done | bytes 65552 | tf_op jit(solution)/shard_map/psum | solution.py:100
  776.9 1.6 copy.58
  (36 shorter events, 1.4 us)
Async XLA Ops:
  7.2 16.3 %all-gather.2.cloned.1.call-start = ((), (), s32[]{:S(2)}) async-start(), calls=%async_computation.2 | async-start | bytes 3145728 | tf_op jit(solution)/shard_map/all_gather | solution.py:52
  9.5 234.0 %reduce-scatter.2.cloned.1.call-start = ((), (), s32[]{:S(2)}) async-start(), calls=%async_computation.3 | async-start | bytes 9437184 | tf_op jit(solution)/shard_map/reduce_scatter | solution.py:54
  95.3 0.8 copy-start.7
  95.3 0.9 copy-start.3
  95.3 148.2 %copy-start.2 = (bf16[128,4096]{1,0:T(8,128)(2,1)S(1)}, bf16[128,4096]{1,0:T(8,128)(2,1)}, u32[]{:S(2)}) copy-start(bf16[128,4096]{1,0:T(8,128)(2,1)} %param.13) | copy-start | bytes 3145732
  95.3 151.0 %copy-start.5 = (s32[32768]{0:T(1024)S(1)}, s32[32768]{0:T(1024)}, u32[]{:S(2)}) copy-start(s32[32768]{0:T(1024)} %constant.66) | copy-start | bytes 393220
  95.4 681.6 %all-reduce.3.cloned.1.call-start = ((), (), s32[]{:S(2)}) async-start(), calls=%async_computation.4 | async-start | bytes 131072 | tf_op jit(solution)/shard_map/psum | solution.py:100
  245.0 154.6 %collective-permute-start.1 = (bf16[128,4096]{1,0:T(8,128)(2,1)S(1)}, bf16[128,4096]{1,0:T(8,128)(2,1)}, u32[]{:S(2)}, u32[]{:S(2)}) collective-permute-start(bf16[128,4096]{1,0:T(8,128)(2,1)S(1)} %fusion.13), channel_id=1, source_target_pairs={{2,0},{4,2},{6,4},{8,6},{10,8},{12,10},{14,12},{3,1},{5,3},{7,5},{... | collective-permute-start | bytes 3145736 | tf_op jit(solution)/shard_map/ppermute | solution.py:11
  375.8 23.5 %copy-start.8 = (s32[1024]{0:T(1024)S(1)}, s32[1024]{0:T(1024)}, u32[]{:S(2)}) copy-start(s32[1024]{0:T(1024)} %param.16) | copy-start | bytes 12292
  417.6 9.3 %copy-start.6 = (pred[128,256]{1,0:T(32,128)(4,1)S(1)}, pred[128,256]{1,0:T(32,128)(4,1)}, u32[]{:S(2)}) copy-start(pred[128,256]{1,0:T(32,128)(4,1)} %constant.45) | copy-start | bytes 98308
  417.6 9.3 %copy-start.4 = (s32[32768]{0:T(1024)S(1)}, s32[32768]{0:T(1024)}, u32[]{:S(2)}) copy-start(s32[32768]{0:T(1024)} %constant.65) | copy-start | bytes 393220
  421.3 159.2 %collective-permute-start = (bf16[128,4096]{1,0:T(8,128)(2,1)}, bf16[128,4096]{1,0:T(8,128)(2,1)}, u32[]{:S(2)}, u32[]{:S(2)}) collective-permute-start(bf16[128,4096]{1,0:T(8,128)(2,1)} %get-tuple-element.11), channel_id=1, source_target_pairs={{0,2},{2,4},{4,6},{6,8},{8,10},{10,12},{12,14},{1,3},{3,5},{5,7},{... | collective-permute-start | bytes 3145736 | tf_op jit(solution)/shard_map/ppermute | solution.py:11
  700.2 9.1 %copy-start = (f32[128,4096]{1,0:T(8,128)S(1)}, f32[128,4096]{1,0:T(8,128)}, u32[]{:S(2)}) copy-start(f32[128,4096]{1,0:T(8,128)} %copy.51) | copy-start | bytes 6291460
  700.2 9.1 %copy-start.1 = (bf16[128,4096]{1,0:T(8,128)(2,1)S(1)}, bf16[128,4096]{1,0:T(8,128)(2,1)}, u32[]{:S(2)}) copy-start(bf16[128,4096]{1,0:T(8,128)(2,1)} %reduce-scatter.2.cloned.1.call-done) | copy-start | bytes 3145732
Sparse Core Ops, SparseCore 0:
  10.1 13.2 all-gather.1
  95.5 148.0 reduce-scatter.1
  709.4 67.4 all-reduce.2
where the time goes:
time: 788 us; the launch traced here: 785 us
  local copies, waits for them, and re-layouts  411 us (52%)
  waiting for transfers between devices  228 us (29%)
  blocking collectives  54.4 us (7%)
  matrix products  51.7 us (7%)
  other arithmetic  19.3 us (2%)
  between operations  13.9 us (2%)
    gather x2, local copies, waits for them, and re-layouts, lag_tables(): jnp.take(filt_vals, np.clip(offsets, 0, tap_count - 1).reshape(-1), axis=1)  259 us
    reduce_scatter x1, waiting for transfers between devices, per_device(): lax.psum_scatter(lax.dot_general(columns, out_weight, (((1,), (1,)), ((),...  147 us
    psum x1, waiting for transfers between devices, per_device(): lax.psum(filt_local.astype(jnp.bfloat16), 'ctx').astype(jnp.float32)  66.4 us
    all_to_all x1, blocking collectives, per_device(): lax.all_to_all(grad_full, 'ctx', split_axis=1, concat_axis=0, tiled=True)  54.4 us
    reshape x2, local copies, waits for them, and re-layouts, lag_tables(): picked = picked.reshape(filt_vals.shape[0], tap_count, 2 * tap_count)  47 us
    reshape x1, local copies, waits for them, and re-layouts, fold_lags(): flat = product.reshape(group_count, 2 * tap_count * tap_count)  35 us
    reshape x1, local copies, waits for them, and re-layouts, fold_lags(): skewed = flat.reshape(group_count, tap_count, 2 * tap_count + 1)  28.3 us
    concatenate x1, local copies, waits for them, and re-layouts, fold_lags(): jnp.concatenate([flat, jnp.zeros((group_count, tap_count), flat.dtype)], 1)  22.4 us
  transfers between devices with their start and end apart: 5, of which 3 were waited for; matrix products, arithmetic and copies ran while one was open for 39% of the time, Pallas kernels for 0%

commit v1 on v0

--- a/solution.py
+++ b/solution.py
@@ -97,7 +97,9 @@
     filt_local = fold_lags(product * prev_masks[block_index].astype(jnp.float32)[None], tap_count)
     key_grad = (grad_parts * value_f32).astype(jnp.bfloat16)
     value_grad = (grad_parts * key_f32).astype(jnp.bfloat16)
-    filter_grad = lax.psum(filt_local.astype(jnp.bfloat16), "ctx").astype(jnp.float32)
+    filter_grad = jnp.sum(
+        lax.all_gather(filt_local.astype(jnp.bfloat16), axis_name="ctx"), axis=0
+    ).astype(jnp.float32)
     return (query_grad, key_grad, value_grad, filter_grad)
 
 

time: 788 us -> 752 us (0.954)
  waiting for transfers between devices: 228 us -> 161 us
  blocking collectives: 54.4 us -> 85.8 us
    psum x1 -> x0, waiting for transfers between devices: 66.4 us -> none  [per_device(): lax.psum(filt_local.astype(jnp.bfloat16), 'ctx').astype(jnp.float32)]
    all_gather x0 -> x1, blocking collectives: none -> 31.4 us  [per_device(): lax.all_gather(filt_local.astype(jnp.bfloat16), axis_name='ctx')]
  transfers between devices with their start and end apart: 5 -> 4, of which waited for: 3 -> 2; matrix products, arithmetic and copies ran while one was open for 39% -> 41% of each run, Pallas kernels for 0% -> 0%
where the time goes in v1:
time: 752 us; the launch traced here: 749 us
  local copies, waits for them, and re-layouts  408 us (54%)
  waiting for transfers between devices  161 us (21%)
  blocking collectives  85.8 us (11%)
  matrix products  51.7 us (7%)
  other arithmetic  21.5 us (3%)
  between operations  14.2 us (2%)
    gather x2, local copies, waits for them, and re-layouts, lag_tables(): jnp.take(filt_vals, np.clip(offsets, 0, tap_count - 1).reshape(-1), axis=1)  258 us
    reduce_scatter x1, waiting for transfers between devices, per_device(): lax.psum_scatter(lax.dot_general(columns, out_weight, (((1,), (1,)), ((),...  147 us
    all_to_all x1, blocking collectives, per_device(): lax.all_to_all(grad_full, 'ctx', split_axis=1, concat_axis=0, tiled=True)  54.4 us
    reshape x2, local copies, waits for them, and re-layouts, lag_tables(): picked = picked.reshape(filt_vals.shape[0], tap_count, 2 * tap_count)  46.6 us
    reshape x1, local copies, waits for them, and re-layouts, fold_lags(): flat = product.reshape(group_count, 2 * tap_count * tap_count)  35 us
    all_gather x1, blocking collectives, per_device(): lax.all_gather(filt_local.astype(jnp.bfloat16), axis_name='ctx')  31.4 us
    reshape x1, local copies, waits for them, and re-layouts, fold_lags(): skewed = flat.reshape(group_count, tap_count, 2 * tap_count + 1)  28.3 us
    concatenate x1, local copies, waits for them, and re-layouts, fold_lags(): jnp.concatenate([flat, jnp.zeros((group_count, tap_count), flat.dtype)], 1)  22.4 us
  transfers between devices with their start and end apart: 4, of which 2 were waited for; matrix products, arithmetic and copies ran while one was open for 41% of the time, Pallas kernels for 0%

profile of v1, /device:TPU:0, one launch (start us, length us, event | category | flops | bytes accessed | tf_op | source)
XLA Modules:
  0.0 749.5 jit_solution(9799485302744497335)
XLA Ops:
  7.2 2.3 copy.58
  9.5 13.9 %all-gather.3.cloned.1.call-done = bf16[128,8192]{0,1:T(8,128)(2,1)} async-done(((bf16[128,4096]{0,1:T(8,128)(2,1)}), bf16[128,8192]{0,1:T(8,128)(2,1)}) %all-gather.3.cloned.1.call-update) | async-done | bytes 2097168 | tf_op jit(solution)/shard_map/all_gather | solution.py:52
  23.4 54.4 %all_to_all.19 = bf16[128,8,1024]{0,2,1:T(8,128)(2,1)S(1)} all-to-all(bf16[128,8,1024]{0,2,1:T(8,128)(2,1)} %bitcast.39), channel_id=1, replica_groups=mesh['group'=2,'ctx'=8,'tp'=2] {'ctx'}, dimensions={1} | all-to-all | bytes 4194304 | tf_op jit(solution)/shard_map/all_to_all | solution.py:53
  77.9 2.6 copy.59
  80.5 14.8 %convolution_convert_fusion = bf16[1024,4096]{1,0:T(8,128)(2,1)} fusion(bf16[1024,1024]{1,0:T(8,128)(2,1)} %bitcast.43, bf16[4096,1024]{1,0:T(8,128)(2,1)} %param.18), kind=kOutput, calls=%fused_computation.16 | convolution fusion | flops 8594128896 | bytes 18874368 | tf_op jit(solution)/shard_map/dot_general | solution.py:55
  95.3 0.7 copy-done.5
  96.3 147.2 %reduce-scatter.2.cloned.1.call-done = bf16[128,4096]{1,0:T(8,128)(2,1)} async-done(((bf16[1024,4096]{1,0:T(8,128)(2,1)}), bf16[128,4096]{1,0:T(8,128)(2,1)}) %reduce-scatter.2.cloned.1.call-update) | async-done | bytes 1048592 | tf_op jit(solution)/shard_map/reduce_scatter | solution.py:54
  243.5 1.5 fusion.13
  245.0 1.3 collective-permute-start.1
  246.3 128.8 %gather_fusion.1 = bf16[32768,256]{1,0:T(8,128)(2,1)} fusion(bf16[256,128]{0,1:T(8,128)(2,1)S(1)} %copy.61, s32[32768]{0:T(1024)S(1)} %broadcast_clamp_fusion), kind=kCustom, calls=%fused_computation.1.clone | custom fusion | bytes 33685504 | tf_op jit(solution)/shard_map/jit(_take)/gather | solution.py:24
  375.1 23.3 %copy.65 = bf16[256,128,256]{2,1,0:T(8,128)(2,1)} copy(bf16[256,128,256]{0,2,1:T(8,128)(2,1)} %bitcast.34) | data formatting | bytes 33554432 | tf_op jit(solution)/shard_map/reshape | solution.py:25
  398.7 1.4 pad_maximum_fusion.1
  400.1 2.5 copy.64
  402.6 12.2 %fusion = f32[256,16,128]{2,1,0:T(8,128)} fusion(bf16[256,256,16]{0,2,1:T(8,128)(2,1)} %bitcast.40, bf16[256,128,256]{2,1,0:T(8,128)(2,1)} %copy.65, pred[128,256]{1,0:T(8,128)(4,1)S(1)} %copy.73, bf16[128,256]{1,0:T(8,128)(2,1)S(1)} %get-tuple-element.16), kind=kOutput, calls=%fused_computation.4 | convolution fusion | flops 285212672 | bytes 21069824 | tf_op jit(solution)/shard_map/gtw,wgc->tgc/dot_general | solution.py:89
  414.8 1.9 copy.66
  416.8 3.7 fusion.14
  420.5 5.6 collective-permute-start
  426.1 128.8 %gather_fusion = bf16[32768,256]{1,0:T(8,128)(2,1)} fusion(bf16[256,128]{0,1:T(8,128)(2,1)S(1)} %copy.61, s32[32768]{0:T(1024)S(1)} %broadcast_clamp_fusion.1), kind=kCustom, calls=%fused_computation.clone | custom fusion | bytes 33685504 | tf_op jit(solution)/shard_map/jit(_take)/gather | solution.py:24
  554.9 23.3 %copy.62 = bf16[256,128,256]{2,1,0:T(8,128)(2,1)} copy(bf16[256,128,256]{0,2,1:T(8,128)(2,1)} %bitcast.33) | data formatting | bytes 33554432 | tf_op jit(solution)/shard_map/reshape | solution.py:25
  578.2 0.7 copy.68
  578.9 3.1 pad_maximum_fusion
  582.0 3.3 copy.60
  585.3 11.6 %fusion.3 = f32[256,16,128]{2,1,0:T(8,128)} fusion(bf16[256,256,16]{0,2,1:T(8,128)(2,1)S(1)} %bitcast.35, bf16[256,128,256]{2,1,0:T(8,128)(2,1)} %copy.62, pred[128,256]{1,0:T(8,128)(4,1)S(1)} %copy.74, bf16[128,256]{1,0:T(8,128)(2,1)S(1)} %get-tuple-element.15), kind=kOutput, calls=%fused_computation.7 | convolution fusion | flops 285212672 | bytes 21069824 | tf_op jit(solution)/shard_map/gtw,wgc->tgc/dot_general | solution.py:74
  596.9 2.9 copy.63
  599.8 3.0 fusion.12
  602.8 13.1 %broadcast_multiply_fusion = f32[256,128,256]{2,1,0:T(8,128)} fusion(f32[128,256]{1,0:T(8,128)S(1)} %get-tuple-element.14, bf16[128,256,16]{0,2,1:T(8,128)(2,1)S(1)} %bitcast.38, bf16[256,256,16]{0,2,1:T(8,128)(2,1)S(1)} %bitcast.36), kind=kOutput, calls=%fused_computation.3 | convolution fusion | flops 276824064 | bytes 36831232 | tf_op jit(solution)/shard_map/tgc,wgc->gtw/dot_general | solution.py:96
  615.9 35.0 %copy.71 = f32[256,128,256]{0,2,1:T(8,128)} copy(f32[256,128,256]{2,1,0:T(8,128)} %broadcast_multiply_fusion) | data formatting | bytes 67108864 | tf_op jit(solution)/shard_map/reshape | solution.py:32
  650.9 22.4 %concatenate.15 = f32[256,32896]{0,1:T(8,128)} pad(f32[256,32768]{0,1:T(8,128)} %bitcast.32, f32[]{:T(128)} %constant.39.clone.1), padding=0_0x0_128 | pad | bytes 67239936 | tf_op jit(solution)/shard_map/concatenate | solution.py:33
  673.4 28.3 %reshape.129 = f32[256,128,257]{0,2,1:T(8,128)} reshape(f32[256,32896]{0,1:T(8,128)} %concatenate.15) | data formatting | bytes 67371008 | tf_op jit(solution)/shard_map/reshape | solution.py:34
  701.6 8.2 %slice_reduce_fusion = bf16[256,128]{0,1:T(8,128)(2,1)S(1)} fusion(f32[256,128,257]{0,2,1:T(8,128)} %reshape.129), kind=kLoop, calls=%fused_computation.2 | loop fusion | flops 4161536 | bytes 16842752 | tf_op jit(solution)/shard_map/reduce_sum | solution.py:35
  710.0 31.4 %all-gather = bf16[2048,128]{0,1:T(8,128)(2,1)S(1)} all-gather(bf16[256,128]{0,1:T(8,128)(2,1)S(1)} %rev.4), channel_id=2, replica_groups=mesh['group'=2,'ctx'=8,'tp'=2] {'ctx'}, dimensions={0}, use_global_device_ids=true | all-gather | bytes 589824 | tf_op jit(solution)/shard_map/all_gather | solution.py:101
  741.9 0.8 copy.70
  (32 shorter events, 1.3 us)
Async XLA Ops:
  7.2 16.3 %all-gather.3.cloned.1.call-start = ((), (), s32[]{:S(2)}) async-start(), calls=%async_computation.2 | async-start | bytes 3145728 | tf_op jit(solution)/shard_map/all_gather | solution.py:52
  9.5 234.0 %reduce-scatter.2.cloned.1.call-start = ((), (), s32[]{:S(2)}) async-start(), calls=%async_computation.3 | async-start | bytes 9437184 | tf_op jit(solution)/shard_map/reduce_scatter | solution.py:54
  95.3 0.8 copy-start.5
  95.3 0.9 copy-start.1
  95.3 148.2 %copy-start = (bf16[128,4096]{1,0:T(8,128)(2,1)S(1)}, bf16[128,4096]{1,0:T(8,128)(2,1)}, u32[]{:S(2)}) copy-start(bf16[128,4096]{1,0:T(8,128)(2,1)} %param.13) | copy-start | bytes 3145732
  95.3 151.0 %copy-start.3 = (s32[32768]{0:T(1024)S(1)}, s32[32768]{0:T(1024)}, u32[]{:S(2)}) copy-start(s32[32768]{0:T(1024)} %constant.67) | copy-start | bytes 393220
  245.0 153.7 %collective-permute-start.1 = (bf16[128,4096]{1,0:T(8,128)(2,1)S(1)}, bf16[128,4096]{1,0:T(8,128)(2,1)}, u32[]{:S(2)}, u32[]{:S(2)}) collective-permute-start(bf16[128,4096]{1,0:T(8,128)(2,1)S(1)} %fusion.13), channel_id=1, source_target_pairs={{2,0},{4,2},{6,4},{8,6},{10,8},{12,10},{14,12},{3,1},{5,3},{7,5},{... | collective-permute-start | bytes 3145736 | tf_op jit(solution)/shard_map/ppermute | solution.py:11
  375.1 23.3 %copy-start.6 = (s32[1024]{0:T(1024)S(1)}, s32[1024]{0:T(1024)}, u32[]{:S(2)}) copy-start(s32[1024]{0:T(1024)} %param.16) | copy-start | bytes 12292
  416.7 9.3 %copy-start.4 = (pred[128,256]{1,0:T(32,128)(4,1)S(1)}, pred[128,256]{1,0:T(32,128)(4,1)}, u32[]{:S(2)}) copy-start(pred[128,256]{1,0:T(32,128)(4,1)} %constant.46) | copy-start | bytes 98308
  416.8 9.3 %copy-start.2 = (s32[32768]{0:T(1024)S(1)}, s32[32768]{0:T(1024)}, u32[]{:S(2)}) copy-start(s32[32768]{0:T(1024)} %constant.66) | copy-start | bytes 393220
  420.5 158.4 %collective-permute-start = (bf16[128,4096]{1,0:T(8,128)(2,1)}, bf16[128,4096]{1,0:T(8,128)(2,1)}, u32[]{:S(2)}, u32[]{:S(2)}) collective-permute-start(bf16[128,4096]{1,0:T(8,128)(2,1)} %get-tuple-element.11), channel_id=1, source_target_pairs={{0,2},{2,4},{4,6},{6,8},{8,10},{10,12},{12,14},{1,3},{3,5},{5,7},{... | collective-permute-start | bytes 3145736 | tf_op jit(solution)/shard_map/ppermute | solution.py:11
Sparse Core Ops, SparseCore 0:
  10.1 13.2 all-gather.2
  95.5 148.0 reduce-scatter.1
